TPU v7x, 32 devices: a whole 2x2x4 slice. The times are simulated.
32 devices in a mesh: seq: 16 (over z, x, core), head: 2 (over y).
Axes of the slice: x: 2, y: 2, z: 4, core: 2. Of those that a mesh axis runs over, the one named last changes fastest.
Arguments:
- features: bfloat16 [8, 32, 8, 512], P(None, 'seq', 'head'), may hold values from -540 to 540
- gn_gain: float32 [512], replicated, may hold values from 0.5 to 1.5
- gn_bias: float32 [512], replicated, may hold values from -3 to 3
- conv_weight: bfloat16 [3, 3, 3, 16, 512], replicated, may hold values from -0.0546875 to 0.0546875
- conv_bias: float32 [16], replicated, may hold values from -3 to 3
- patch_weight: bfloat16 [64, 3072], replicated, may hold values from -0.75 to 0.75
- patch_bias: float32 [3072], replicated, may hold values from -3 to 3
- image_mod: float32 [3, 3072], replicated, may hold values from -3 to 3
- w_qkv: bfloat16 [3072, 3, 2048], P('seq', None, 'head'), may hold values from -5 to 5
- text_ids: int32 [512], replicated, may hold values from 0 to 16383
- text_length: int32 [1], replicated, may hold values from 256 to 512
- text_table: bfloat16 [3072, 16384], P('seq'), may hold values from -60 to 60
- text_mod: float32 [2, 3072], P(None, 'seq'), may hold values from -3 to 3
- w_text: bfloat16 [3072, 2, 2048], P('seq', None, 'head'), may hold values from -2 to 2
- w_out: bfloat16 [2048, 3072], P('head'), may hold values from -0.625 to 0.625
- out_bias: float32 [3072], replicated, may hold values from -3 to 3
Outputs:
- block_out: bfloat16 [8, 16, 4, 3072], P(None, 'seq', 'head')
All inputs are finite; a program needn't handle non-finite values.
Results may differ from a plain program's by a relative error of at most 0.0089.
Values may be sent and summed in bfloat16 or wider, within the bound.
A program may use at most 128 MiB of HBM per device.

v0:
```python
import jax
import jax.numpy as jnp
from jax import lax
from jax.sharding import PartitionSpec as P

HD = 128
GN_GROUPS = 32
CHUNK = 512
eps_norm = 1e-06


def group_gather(piece, group, dim):
    if group == 1:
        return piece
    count = lax.axis_size("seq")
    if group == 2:
        other = lax.ppermute(piece, "seq", [(i, i ^ 1) for i in range(count)])
        first = lax.axis_index("seq") % 2 == 0
        return jnp.concatenate(
            [jnp.where(first, piece, other), jnp.where(first, other, piece)], axis=dim
        )
    members = [list(range(i, i + group)) for i in range(0, count, group)]
    return lax.all_gather(piece, "seq", axis=dim, tiled=True, axis_index_groups=members)


def group_norm(features, gn_gain, gn_bias):
    frame_count, row_count, col_count, chan_count = features.shape
    per_group = chan_count // GN_GROUPS
    values = features.astype(jnp.float32)
    chan_sums = jnp.stack(
        [jnp.sum(values, axis=(0, 1, 2)), jnp.sum(values * values, axis=(0, 1, 2))]
    )
    sums = jnp.sum(chan_sums.reshape(2, GN_GROUPS, per_group), axis=2)
    sums = lax.psum(sums, ("seq", "head"))
    cell_count = (
        frame_count
        * row_count
        * col_count
        * per_group
        * lax.axis_size("seq")
        * lax.axis_size("head")
    )
    mean = sums[0] / cell_count
    scale = lax.rsqrt(sums[1] / cell_count - mean * mean + eps_norm)
    mean = jnp.repeat(mean, per_group)
    scale = jnp.repeat(scale, per_group)
    normed = (values - mean) * scale
    return jax.nn.silu(normed * gn_gain + gn_bias).astype(jnp.bfloat16)


def join_rims(parts, block_dim, dim, unit):
    size = parts.shape[dim]
    blocks = parts.shape[block_dim]
    core = lax.slice_in_dim(parts, unit, size - unit, axis=dim)
    low = lax.slice_in_dim(parts, 0, unit, axis=dim)
    high = lax.slice_in_dim(parts, size - unit, size, axis=dim)
    low = lax.slice_in_dim(low, 1, blocks, axis=block_dim)
    high = lax.slice_in_dim(high, 0, blocks - 1, axis=block_dim)
    pad_low = [(0, 0)] * parts.ndim
    pad_low[block_dim] = (0, 1)
    pad_low[dim] = (size - 3 * unit, 0)
    pad_high = [(0, 0)] * parts.ndim
    pad_high[block_dim] = (1, 0)
    pad_high[dim] = (0, size - 3 * unit)
    return core + jnp.pad(low, pad_low) + jnp.pad(high, pad_high)


def all_patches(activated, conv_weight, conv_bias):
    seq_n, head_n = (lax.axis_size("seq"), lax.axis_size("head"))
    frame_count, row_count, col_count, _ = activated.shape
    chans = conv_weight.shape[3]
    padded = jnp.concatenate([activated[:1], activated[:1], activated], axis=0)
    shares = lax.conv_general_dilated(
        padded[None],
        conv_weight,
        (1, 1, 1),
        ((0, 0), (2, 2), (2, 2)),
        dimension_numbers=("NDHWC", "DHWOI", "NDHWC"),
        preferred_element_type=jnp.float32,
    )[0]
    flat = shares.reshape(-1, 128)
    parts = lax.all_gather(flat, ("seq", "head"), axis=0, tiled=False)
    parts = parts.reshape(seq_n, head_n, frame_count, row_count + 2, (col_count + 2) * chans)
    parts = join_rims(join_rims(parts, 0, 3, 1), 1, 4, chans)
    latent = (parts + jnp.tile(conv_bias, col_count)).astype(jnp.bfloat16)
    blocks = latent.reshape(
        seq_n, head_n, frame_count, row_count // 2, 2, col_count // 2, 2 * chans
    )
    blocks = blocks.transpose(0, 1, 2, 3, 5, 4, 6)
    own = frame_count * (row_count // 2) * (col_count // 2)
    return blocks.reshape(seq_n * head_n * own, 4 * chans)


def modulate(patches, patch_weight, patch_bias, image_mod):
    hidden = jnp.dot(patches, patch_weight, preferred_element_type=jnp.float32) + patch_bias
    center = jnp.mean(hidden, axis=1, keepdims=True)
    offset = hidden - center
    spread = jnp.mean(offset * offset, axis=1, keepdims=True)
    normed = offset * lax.rsqrt(spread + eps_norm)
    return (normed * (1.0 + image_mod[1]) + image_mod[0]).astype(jnp.bfloat16)


def body(
    features,
    gn_gain,
    gn_bias,
    conv_weight,
    conv_bias,
    patch_weight,
    patch_bias,
    image_mod,
    w_qkv,
    text_ids,
    text_length,
    text_table,
    text_mod,
    w_text,
    w_out,
    out_bias,
):
    frame_count, row_count, col_count, _ = features.shape
    width_full = patch_weight.shape[1]
    seq_n, head_n = (lax.axis_size("seq"), lax.axis_size("head"))
    seq_i, head_i = (lax.axis_index("seq"), lax.axis_index("head"))
    depth, _, head_width = w_qkv.shape
    heads_here = head_width // HD
    group = seq_n // heads_here
    cols = head_width // seq_n
    text_count = text_ids.shape[0]
    both = jnp.concatenate([w_qkv, w_text], axis=1).reshape(depth, 5, seq_n, cols)
    both = both.transpose(2, 0, 1, 3).reshape(seq_n, depth, 5 * cols)
    both = lax.all_to_all(both, "seq", split_axis=0, concat_axis=0, tiled=True)
    both = both.reshape(seq_n * depth, 5, cols)
    both = group_gather(both, group, 2)
    w_query, w_image, w_text_full = (both[:, 0], both[:, 1:3], both[:, 3:5])
    chosen = (
        lax.broadcasted_iota(jnp.int32, (text_table.shape[1], text_count), 0) == text_ids[None, :]
    ).astype(jnp.bfloat16)
    own_context = jnp.dot(text_table, chosen, preferred_element_type=jnp.float32).astype(
        jnp.bfloat16
    )
    context = lax.all_gather(own_context, "seq", axis=0, tiled=True).astype(jnp.float32)
    mod = lax.all_gather(text_mod, "seq", axis=1, tiled=True)
    text_mean = jnp.sum(context, axis=0) / width_full
    text_square = jnp.sum(context * context, axis=0) / width_full
    text_scale = lax.rsqrt(text_square - text_mean * text_mean + eps_norm)
    text_normed = (context - text_mean) * text_scale * (1.0 + mod[1][:, None]) + mod[0][:, None]
    text_high = text_normed.astype(jnp.bfloat16)
    text_low = (text_normed - text_high.astype(jnp.float32)).astype(jnp.bfloat16)
    w_text_flat = w_text_full.reshape(width_full, 2 * HD)
    text_kv = sum(
        (
            lax.dot_general(
                part, w_text_flat, (((0,), (0,)), ((), ())), preferred_element_type=jnp.float32
            )
            for part in (text_high, text_low)
        )
    ).astype(jnp.bfloat16)
    activated = group_norm(features, gn_gain, gn_bias)
    patches = all_patches(activated, conv_weight, conv_bias)
    own = patches.shape[0] // (seq_n * head_n)
    part_rows = head_n * own // group
    my_part = seq_i % group
    chunk = min(CHUNK, patches.shape[0])

    def project(rows):
        modulated = modulate(rows, patch_weight, patch_bias, image_mod)
        kv = jnp.dot(
            modulated, w_image.reshape(width_full, 2 * HD), preferred_element_type=jnp.float32
        )
        query = jnp.dot(modulated, w_query, preferred_element_type=jnp.float32)
        query = lax.dynamic_index_in_dim(
            query.reshape(-1, group, part_rows, HD), my_part, axis=1, keepdims=False
        )
        return (kv.astype(jnp.bfloat16), query.reshape(-1, HD).astype(jnp.bfloat16))

    if chunk == patches.shape[0]:
        image_kv, query = project(patches)
    else:
        image_kv, query = lax.map(project, patches.reshape(-1, chunk, patches.shape[1]))
        image_kv = image_kv.reshape(-1, 2 * HD)
        query = query.reshape(-1, HD)
    keys = jnp.concatenate([image_kv[:, :HD], text_kv[:, :HD]], axis=0)
    vals = jnp.concatenate([image_kv[:, HD:], text_kv[:, HD:]], axis=0)
    key_valid = jnp.arange(keys.shape[0], dtype=jnp.int32) < image_kv.shape[0] + text_length[0]
    scores = (
        lax.dot_general(query, keys, (((1,), (1,)), ((), ())), preferred_element_type=jnp.float32)
        / HD
    )
    scores = jnp.where(key_valid[None, :], scores, -1e30)
    probs = jnp.exp(scores - jnp.max(scores, axis=1, keepdims=True))
    totals = jnp.sum(probs, axis=1, keepdims=True)
    attended = (
        jnp.dot(probs.astype(jnp.bfloat16), vals, preferred_element_type=jnp.float32) / totals
    ).astype(jnp.bfloat16)
    attended = attended.reshape(seq_n, part_rows, HD)
    attended = lax.all_to_all(attended, "seq", split_axis=0, concat_axis=0, tiled=True)
    attended = attended.reshape(heads_here, group, part_rows, HD).transpose(1, 2, 0, 3)
    attended = attended.reshape(head_n * own, head_width)
    if head_n == 2:
        halves = attended.reshape(2, own, head_width)
        away = jnp.dot(
            lax.dynamic_index_in_dim(halves, 1 - head_i, 0, keepdims=False),
            w_out,
            preferred_element_type=jnp.float32,
        )
        here = jnp.dot(
            lax.dynamic_index_in_dim(halves, head_i, 0, keepdims=False),
            w_out,
            preferred_element_type=jnp.float32,
        )
        projected = here + lax.ppermute(away, "head", [(0, 1), (1, 0)]) + out_bias
    else:
        projected = (
            lax.psum_scatter(
                jnp.dot(attended, w_out, preferred_element_type=jnp.float32),
                "head",
                scatter_dimension=0,
                tiled=True,
            )
            + out_bias
        )
    own_patches = lax.dynamic_slice_in_dim(patches, (seq_i * head_n + head_i) * own, own, axis=0)
    hidden = jnp.dot(own_patches, patch_weight, preferred_element_type=jnp.float32) + patch_bias
    block_out = (hidden + image_mod[2] * projected).astype(jnp.bfloat16)
    return block_out.reshape(frame_count, row_count // 2, col_count // 2, width_full)


def solution(mesh):
    return jax.shard_map(
        body,
        mesh=mesh,
        in_specs=(
            P(None, "seq", "head", None),
            P(),
            P(),
            P(),
            P(),
            P(),
            P(),
            P(),
            P("seq", None, "head"),
            P(),
            P(),
            P("seq", None),
            P(None, "seq"),
            P("seq", None, "head"),
            P("head", None),
            P(),
        ),
        out_specs=P(None, "seq", "head", None),
        check_vma=False,
    )
```

profile of v0, /device:TPU:0, one launch (start us, length us, event | category | flops | bytes accessed | tf_op | source)
XLA Modules:
  0.0 296.0 jit_solution(9451545067675089896)
XLA Ops:
  6.5 2.5 copy.83
  9.0 1.6 copy.82
  10.7 0.4 pad_maximum_fusion
  11.1 0.2 copy.84
  11.3 2.6 copy.85
  13.9 7.4 %all-to-all-start = ((bf16[16,192,320]{2,1,0:T(8,128)(2,1)}), bf16[16,192,320]{2,1,0:T(8,128)(2,1)}, u32[]{:S(2)}, u32[]{:S(2)}) async-start(bf16[16,192,320]{2,1,0:T(8,128)(2,1)} %copy.85), calls=%async_computation | async-start | bytes 4718592 | tf_op jit(solution)/shard_map/all_to_all | solution.py:132
  21.4 0.0 all-gather.3.cloned.1.call-start
  21.5 9.1 %fusion.23 = bf16[192,512]{1,0:T(8,128)(2,1)} fusion(bf16[192,16384]{1,0:T(8,128)(2,1)} %param.27, s32[512]{0:T(512)S(1)} %copy-done.19), kind=kOutput, calls=%fused_computation.34 | convolution fusion | flops 3229712384 | bytes 6490112 | tf_op jit(solution)/shard_map/dot_general | solution.py:139
  30.6 0.0 all-gather.3.cloned.1.call-update
  30.6 0.1 convert_reduce_fusion.1
  30.7 0.1 stack.10
  30.8 0.1 stack.9
  30.9 0.1 maximum_reduce_fusion
  31.0 83.9 %psum.7 = f32[2,32]{1,0:T(2,128)S(1)} all-reduce(f32[2,32]{1,0:T(2,128)S(1)} %maximum_reduce_fusion), channel_id=1, replica_groups=mesh['seq'=16,'head'=2] {'seq','head'}, use_global_device_ids=true, to_apply=%region_3.4 | all-reduce | flops 64 | bytes 512 | tf_op jit(solution)/shard_map/psum | solution.py:34
  114.8 0.1 broadcast_in_dim.15
  114.9 0.1 mul.93
  115.0 0.1 broadcast_in_dim.14
  115.1 0.1 sub.50
  115.2 0.1 fusion.50
  115.3 0.1 maximum_bitcast_fusion.2
  115.4 4.2 %convolution_reduce_fusion = f32[8,4,6,16]{3,2,1,0:T(8,128)S(1)} fusion(bf16[3,3,3,16,512]{4,3,2,1,0:T(8,128)(2,1)S(1)} %copy-done, bf16[1,10,2,4,512]{4,3,2,1,0:T(4,128)(2,1)S(1)} %maximum_bitcast_fusion.2), kind=kOutput, calls=%fused_computation.36 | convolution fusion | flops 28311552 | bytes 536576 | tf_op jit(solution)/shard_map/conv_general_dilated | solution.py:73
  119.6 0.1 all_gather_reshape_squeeze.3
  119.7 68.1 %all_gather.9 = f32[32,24,128]{2,1,0:T(8,128)S(1)} all-gather(f32[1,24,128]{2,1,0:T(8,128)S(1)} %all_gather_reshape_squeeze.3), channel_id=1, replica_groups=mesh['seq'=16,'head'=2] {'seq','head'}, dimensions={0}, use_global_device_ids=true | all-gather | bytes 405504 | tf_op jit(solution)/shard_map/all_gather | solution.py:82
  187.9 0.3 reshape.98
  188.2 0.1 slice.94
  188.4 0.1 add.179
  188.4 0.2 fusion.65
  188.7 0.1 fusion.68
  188.8 0.2 fusion.34
  189.0 0.1 reshape.99
  189.1 0.3 copy.81
  189.4 0.1 reshape.100
  189.6 3.6 %add_reduce_fusion = (f32[512]{0:T(512)S(1)}, f32[512,3072]{1,0:T(8,128)}) fusion(f32[3072]{0:T(1024)S(1)} %copy-done.11, bf16[512,64]{1,0:T(8,128)(2,1)S(1)} %reshape.100, bf16[64,3072]{1,0:T(8,128)(2,1)S(1)} %copy-done.7), kind=kOutput, calls=%fused_computation.15 | convolution fusion | flops 204471808 | bytes 6764544 | tf_op jit(solution)/shard_map/dot_general | solution.py:95
  193.2 17.4 %all-gather = f32[16,192,2]{1,2,0:T(2,128)S(1)} all-gather(f32[1,192,2]{1,2,0:T(2,128)S(1)} %bitcast.101), channel_id=1, replica_groups=mesh['seq'=16,'head'=2] {'seq'}, dimensions={0}, use_global_device_ids=true | all-gather | bytes 26112 | tf_op jit(solution)/shard_map/all_gather | solution.py:143
  210.6 0.1 reshape.110
  210.8 3.9 %copy.86 = bf16[16,192,320]{1,0,2:T(8,128)(2,1)S(1)} copy(bf16[16,192,320]{2,1,0:T(8,128)(2,1)} %all-to-all-done) | data formatting | bytes 3932160 | tf_op jit(solution)/shard_map/all_to_all | solution.py:132
  214.7 3.7 %reshape.103 = bf16[3072,5,64]{0,2,1:T(8,128)(2,1)} reshape(bf16[16,192,320]{1,0,2:T(8,128)(2,1)S(1)} %copy.86) | data formatting | bytes 3932160 | tf_op jit(solution)/shard_map/reshape | solution.py:133
  218.4 0.3 collective-permute-start
  218.7 3.7 %multiply_reduce_fusion = f32[512]{0:T(512)S(1)} fusion(f32[512,3072]{1,0:T(8,128)} %get-tuple-element.29, f32[512]{0:T(512)S(1)} %broadcast_multiply_fusion.1, f32[3072]{0:T(1024)S(1)} %copy-done.11), kind=kLoop, calls=%fused_computation.14 | loop fusion | flops 6290944 | bytes 6307840 | tf_op jit(solution)/shard_map/reduce_sum | solution.py:98
  223.2 6.3 %add_convert_fusion = bf16[512,3072]{1,0:T(8,128)(2,1)} fusion(f32[512,3072]{1,0:T(8,128)} %get-tuple-element.29, f32[3072]{0:T(1024)S(1)} %bitcast.95, f32[3072]{0:T(1024)S(1)} %bitcast.96, f32[512]{0:T(512)S(1)} %add_rsqrt_fusion.1, f32[512]{0:T(512)S(1)} %broadcast_multiply_fusion.1, f32[3072]{0:T(1024)S(1)} %copy-done.11), kind=kLoop, calls=%fused_computation.13 | loop fusion | flops 9437184 | bytes 9478144 | tf_op jit(solution)/shard_map/convert_element_type | solution.py:100
  229.5 3.1 %copy.87 = bf16[3072,5,64]{2,0,1:T(8,128)(2,1)} copy(bf16[3072,5,64]{0,2,1:T(8,128)(2,1)S(1)} %copy-done.5) | data formatting | bytes 3932160 | tf_op jit(solution)/shard_map/reshape | solution.py:133
  232.6 4.7 %copy.88 = bf16[3072,5,64]{2,0,1:T(8,128)(2,1)} copy(bf16[3072,5,64]{0,2,1:T(8,128)(2,1)} %collective-permute-done) | data formatting | bytes 3932160 | tf_op jit(solution)/shard_map/ppermute | solution.py:17
  237.3 3.6 %broadcast_select_fusion.1 = (bf16[3072,5,64]{2,0,1:T(8,128)(2,1)S(1)}, bf16[3072,5,64]{2,0,1:T(8,128)(2,1)S(1)}) fusion(bf16[3072,5,64]{2,0,1:T(8,128)(2,1)} %copy.87, bf16[3072,5,64]{2,0,1:T(8,128)(2,1)} %copy.88, pred[]{:T(512)S(6)} %eq.14), kind=kLoop, calls=%fused_computation.17 | loop fusion | flops 1966080 | bytes 7864321 | tf_op jit(solution)/shard_map/jit(_where)/select_n | solution.py:20
  240.9 3.3 %pad_maximum_fusion.2 = (bf16[3072,2,128]{2,0,1:T(8,128)(2,1)S(1)}, bf16[3072,2,128]{2,0,1:T(8,128)(2,1)}) fusion(bf16[3072,5,64]{2,0,1:T(8,128)(2,1)S(1)} %get-tuple-element.12, bf16[3072,5,64]{2,0,1:T(8,128)(2,1)S(1)} %get-tuple-element.11), kind=kLoop, calls=%fused_computation.27 | loop fusion | flops 6291456 | bytes 7077888 | tf_op jit(solution)/shard_map/slice | solution.py:135
  244.3 0.2 copy-done.3
  244.4 2.6 copy.93
  247.0 1.6 copy.91
  248.6 3.5 %fusion.27 = bf16[16,2,16,128]{3,2,1,0:T(8,128)(2,1)S(1)} fusion(bf16[16,2,16,3072]{3,2,1,0:T(8,128)(2,1)} %bitcast.80, bf16[3072,5,64]{2,0,1:T(8,128)(2,1)} %copy-done.3, bf16[3072,5,64]{2,0,1:T(8,128)(2,1)} %copy-done.2), kind=kOutput, calls=%fused_computation.42 | convolution fusion | flops 404226048 | bytes 7208960 | tf_op jit(solution)/shard_map/dot_general | solution.py:171
  252.2 0.2 copy-done.9
  252.4 1.0 convolution_convert_fusion
  253.4 0.0 all-gather.3.cloned.1.call-done
  253.5 2.8 convert_reduce_fusion
  256.2 4.0 %fusion.43 = f32[512,256]{1,0:T(8,128)S(1)} fusion(bf16[3072,256]{0,1:T(8,128)(2,1)S(1)} %bitcast.83, bf16[3072,512]{1,0:T(8,128)(2,1)} %all-gather.3.cloned.1.call-done, f32[3072]{0:T(1024)S(1)} %bitcast.99, f32[3072]{0:T(1024)S(1)} %bitcast.97, f32[512]{0:T(512)S(1)} %get-tuple-element.27, f32[512]{0:T(512)S(1)} %get-tuple-element.26), kind=kOutput, calls=%fused_computation.58 | convolution fusion | flops 814743552 | bytes 5271552 | tf_op jit(solution)/shard_map/dot_general | solution.py:153
  260.3 2.1 fusion.19
  262.4 0.4 fusion.70
  262.8 0.3 fusion.25
  263.1 1.0 fusion.24
  264.1 3.6 %all-to-all-start.1 = ((bf16[16,16,128]{2,1,0:T(8,128)(2,1)}), bf16[16,16,128]{2,1,0:T(8,128)(2,1)S(1)}, u32[]{:S(2)}, u32[]{:S(2)}) async-start(bf16[16,16,128]{2,1,0:T(8,128)(2,1)} %bitcast.24), calls=%async_computation.1 | async-start | bytes 131072 | tf_op jit(solution)/shard_map/all_to_all | solution.py:197
  267.7 6.8 %all-to-all-done.1 = bf16[16,16,128]{2,1,0:T(8,128)(2,1)S(1)} async-done(((bf16[16,16,128]{2,1,0:T(8,128)(2,1)}), bf16[16,16,128]{2,1,0:T(8,128)(2,1)S(1)}, u32[]{:S(2)}, u32[]{:S(2)}) %all-to-all-start.1) | async-done | bytes 65568 | tf_op jit(solution)/shard_map/all_to_all | solution.py:197
  274.6 3.8 %fusion.51 = f32[16,3072]{1,0:T(8,128)S(1)} fusion(bf16[1024,3072]{1,0:T(8,128)(2,1)} %param.30, bf16[2,16,1024]{2,1,0:T(8,128)(2,1)S(1)} %bitcast.89, s32[]{:T(128)S(6)} %select_n.47), kind=kOutput, calls=%fused_computation.73 | convolution fusion | flops 100663296 | bytes 6520836 | tf_op jit(solution)/shard_map/dot_general | solution.py:202
  278.4 0.9 convolution_add_fusion
  279.2 5.5 %collective-permute-done.1 = f32[16,3072]{1,0:T(8,128)S(1)} collective-permute-done((f32[16,3072]{1,0:T(8,128)S(1)}, f32[16,3072]{1,0:T(8,128)S(1)}, u32[]{:S(2)}, u32[]{:S(2)}) %collective-permute-start.1) | collective-permute-done | bytes 196640 | tf_op jit(solution)/shard_map/ppermute | solution.py:212
  284.8 3.7 %fusion.12 = bf16[16,3072]{1,0:T(8,128)(2,1)S(1)} fusion(f32[16,3072]{1,0:T(8,128)S(1)} %convolution_add_fusion, f32[16,3072]{1,0:T(8,128)S(1)} %collective-permute-done.1, bf16[1024,3072]{1,0:T(8,128)(2,1)} %param.30, f32[3072]{0:T(1024)S(1)} %copy-done.14, f32[3072]{0:T(1024)S(1)} %bitcast.94, bf16[2,16,1024]{2,1,0:T(8,128)(2,1)S(1)} %bitcast.90, ...), kind=kOutput, calls=%fused_computation.23 | convolution fusion | flops 100909056 | bytes 6840324 | tf_op jit(solution)/shard_map/dot_general | solution.py:207
  288.5 0.7 reshape.108
  (57 shorter events, 0.3 us)
Async XLA Ops:
  6.5 108.8 %copy-start = (bf16[3,3,3,16,512]{4,3,2,1,0:T(8,128)(2,1)S(1)}, bf16[3,3,3,16,512]{4,3,2,1,0:T(8,128)(2,1)}, u32[]{:S(2)}) copy-start(bf16[3,3,3,16,512]{4,3,2,1,0:T(8,128)(2,1)} %param.19) | copy-start | bytes 1327108
  11.3 10.1 %copy-start.19 = (s32[512]{0:T(512)S(1)}, s32[512]{0:T(512)}, u32[]{:S(2)}) copy-start(s32[512]{0:T(512)} %param.25) | copy-start | bytes 6148
  13.9 196.8 %all-to-all-start = ((bf16[16,192,320]{2,1,0:T(8,128)(2,1)}), bf16[16,192,320]{2,1,0:T(8,128)(2,1)}, u32[]{:S(2)}, u32[]{:S(2)}) async-start(bf16[16,192,320]{2,1,0:T(8,128)(2,1)} %copy.85), calls=%async_computation | async-start | bytes 4718592 | tf_op jit(solution)/shard_map/all_to_all | solution.py:132
  21.4 9.3 %copy-start.12 = (bf16[8,2,4,512]{3,2,1,0:T(4,128)(2,1)S(1)}, bf16[8,2,4,512]{3,2,1,0:T(4,128)(2,1)}, u32[]{:S(2)}) copy-start(bf16[8,2,4,512]{3,2,1,0:T(4,128)(2,1)} %param.16) | copy-start | bytes 196612
  21.4 93.8 %copy-start.15 = (f32[512]{0:T(512)S(1)}, f32[512]{0:T(512)}, u32[]{:S(2)}) copy-start(f32[512]{0:T(512)} %param.18) | copy-start | bytes 6148
  21.4 93.8 %copy-start.16 = (f32[512]{0:T(512)S(1)}, f32[512]{0:T(512)}, u32[]{:S(2)}) copy-start(f32[512]{0:T(512)} %param.17) | copy-start | bytes 6148
  21.4 167.0 %copy-start.18 = (f32[16]{0:T(128)S(1)}, f32[16]{0:T(128)}, u32[]{:S(2)}) copy-start(f32[16]{0:T(128)} %param.20) | copy-start | bytes 196
  21.4 232.0 %all-gather.3.cloned.1.call-start = ((), (), s32[]{:S(2)}) async-start(), calls=%async_computation.2 | async-start | bytes 3342336 | tf_op jit(solution)/shard_map/all_gather | solution.py:142
  30.6 158.9 %copy-start.7 = (bf16[64,3072]{1,0:T(8,128)(2,1)S(1)}, bf16[64,3072]{1,0:T(8,128)(2,1)}, u32[]{:S(2)}) copy-start(bf16[64,3072]{1,0:T(8,128)(2,1)} %param.21) | copy-start | bytes 1179652
  30.6 158.9 %copy-start.11 = (f32[3072]{0:T(1024)S(1)}, f32[3072]{0:T(1024)}, u32[]{:S(2)}) copy-start(f32[3072]{0:T(1024)} %param.22) | copy-start | bytes 36868
  189.5 3.7 %copy-start.10 = (bf16[512,64]{1,0:T(8,128)(2,1)}, bf16[512,64]{1,0:T(8,128)(2,1)S(1)}, u32[]{:S(2)}) copy-start(bf16[512,64]{1,0:T(8,128)(2,1)S(1)} %reshape.100) | copy-start | bytes 196612
  189.6 3.6 %copy-start.17 = (f32[2,192]{1,0:T(2,128)S(1)}, f32[2,192]{1,0:T(2,128)}, u32[]{:S(2)}) copy-start(f32[2,192]{1,0:T(2,128)} %param.28) | copy-start | bytes 4612
  218.4 4.7 %copy-start.13 = (f32[3,3072]{1,0:T(4,128)S(1)}, f32[3,3072]{1,0:T(4,128)}, u32[]{:S(2)}) copy-start(f32[3,3072]{1,0:T(4,128)} %param.23) | copy-start | bytes 110596
  218.4 14.2 %collective-permute-start = (bf16[3072,5,64]{0,2,1:T(8,128)(2,1)}, bf16[3072,5,64]{0,2,1:T(8,128)(2,1)}, u32[]{:S(2)}, u32[]{:S(2)}) collective-permute-start(bf16[3072,5,64]{0,2,1:T(8,128)(2,1)} %reshape.103), channel_id=1, source_target_pairs={{0,2},{2,0},{4,6},{6,4},{8,10},{10,8},{12,14},{14,12},{16,18},{18,... | collective-permute-start | bytes 5898248 | tf_op jit(solution)/shard_map/ppermute | solution.py:17
  223.2 6.3 %copy-start.5 = (bf16[3072,5,64]{0,2,1:T(8,128)(2,1)S(1)}, bf16[3072,5,64]{0,2,1:T(8,128)(2,1)}, u32[]{:S(2)}) copy-start(bf16[3072,5,64]{0,2,1:T(8,128)(2,1)} %reshape.103) | copy-start | bytes 5898244
  240.9 3.4 %copy-start.2 = (bf16[3072,5,64]{2,0,1:T(8,128)(2,1)}, bf16[3072,5,64]{2,0,1:T(8,128)(2,1)S(1)}, u32[]{:S(2)}) copy-start(bf16[3072,5,64]{2,0,1:T(8,128)(2,1)S(1)} %get-tuple-element.11) | copy-start | bytes 5898244
  240.9 3.5 %copy-start.3 = (bf16[3072,5,64]{2,0,1:T(8,128)(2,1)}, bf16[3072,5,64]{2,0,1:T(8,128)(2,1)S(1)}, u32[]{:S(2)}) copy-start(bf16[3072,5,64]{2,0,1:T(8,128)(2,1)S(1)} %get-tuple-element.12) | copy-start | bytes 5898244
  248.6 3.6 %copy-start.4 = (bf16[512,3072]{1,0:T(8,128)(2,1)S(1)}, bf16[512,3072]{1,0:T(8,128)(2,1)}, u32[]{:S(2)}) copy-start(bf16[512,3072]{1,0:T(8,128)(2,1)} %add_convert_fusion) | copy-start | bytes 9437188
  248.6 3.8 %copy-start.9 = (bf16[3072,2,128]{0,2,1:T(8,128)(2,1)S(1)}, bf16[3072,2,128]{0,2,1:T(8,128)(2,1)}, u32[]{:S(2)}) copy-start(bf16[3072,2,128]{0,2,1:T(8,128)(2,1)} %copy.91) | copy-start | bytes 4718596
  252.4 3.9 %copy-start.8 = (bf16[3072,2,128]{0,2,1:T(8,128)(2,1)S(1)}, bf16[3072,2,128]{0,2,1:T(8,128)(2,1)}, u32[]{:S(2)}) copy-start(bf16[3072,2,128]{0,2,1:T(8,128)(2,1)} %copy.93) | copy-start | bytes 4718596
  256.2 4.0 %copy-start.6 = (bf16[3072,512]{1,0:T(8,128)(2,1)S(1)}, bf16[3072,512]{1,0:T(8,128)(2,1)}, u32[]{:S(2)}) copy-start(bf16[3072,512]{1,0:T(8,128)(2,1)} %all-gather.3.cloned.1.call-done) | copy-start | bytes 9437188
  264.1 20.7 %copy-start.14 = (f32[3072]{0:T(1024)S(1)}, f32[3072]{0:T(1024)}, u32[]{:S(2)}) copy-start(f32[3072]{0:T(1024)} %param.31) | copy-start | bytes 36868
  264.1 10.5 %all-to-all-start.1 = ((bf16[16,16,128]{2,1,0:T(8,128)(2,1)}), bf16[16,16,128]{2,1,0:T(8,128)(2,1)S(1)}, u32[]{:S(2)}, u32[]{:S(2)}) async-start(bf16[16,16,128]{2,1,0:T(8,128)(2,1)} %bitcast.24), calls=%async_computation.1 | async-start | bytes 131072 | tf_op jit(solution)/shard_map/all_to_all | solution.py:197
  274.6 14.6 %copy-start.1 = (bf16[3,3,3,16,512]{4,3,2,1,0:T(8,128)(2,1)S(1)}, bf16[3,3,3,16,512]{4,3,2,1,0:T(8,128)(2,1)}, u32[]{:S(2)}) copy-start(bf16[3,3,3,16,512]{4,3,2,1,0:T(8,128)(2,1)} %param.19) | copy-start | bytes 1327108
  278.4 6.4 %collective-permute-start.1 = (f32[16,3072]{1,0:T(8,128)S(1)}, f32[16,3072]{1,0:T(8,128)S(1)}, u32[]{:S(2)}, u32[]{:S(2)}) collective-permute-start(f32[16,3072]{1,0:T(8,128)S(1)} %fusion.51), channel_id=1, source_target_pairs={{0,1},{1,0},{2,3},{3,2},{4,5},{5,4},{6,7},{7,6},{8,9},{9,8},{10,11... | collective-permute-start | bytes 589832 | tf_op jit(solution)/shard_map/ppermute | solution.py:212
Sparse Core Ops, SparseCore 0:
  30.8 66.3 all-gather.2
where the time goes:
time: 297 us; the launch traced here: 296 us
  blocking collectives  169 us (57%)
  matrix products  37.4 us (13%)
  local copies, waits for them, and re-layouts  29.8 us (10%)
  other arithmetic  21.1 us (7%)
  between operations  14.6 us (5%)
  waiting for transfers between devices  12.4 us (4%)
  starting transfers between devices  11.4 us (4%)
    psum x1, blocking collectives, group_norm(): sums = lax.psum(sums, ('seq', 'head'))  83.9 us
    all_gather x1, blocking collectives, all_patches(): parts = lax.all_gather(flat, ('seq', 'head'), axis=0, tiled=False)  68.1 us
    all_gather x1, blocking collectives, body(): mod = lax.all_gather(text_mod, 'seq', axis=1, tiled=True)  17.4 us
    dot_general x1, matrix products, body(): jnp.dot(text_table, chosen, preferred_element_type=jnp.float32)  9.15 us
    all_to_all x1, starting transfers between devices, body(): both = lax.all_to_all(both, 'seq', split_axis=0, concat_axis=0, tiled=True)  7.4 us
    all_to_all x1, waiting for transfers between devices, body(): lax.all_to_all(attended, 'seq', split_axis=0, concat_axis=0, tiled=True)  6.85 us
    reshape x2, local copies, waits for them, and re-layouts, body(): both = both.reshape(seq_n * depth, 5, cols)  6.84 us
    convert_element_type x1, other arithmetic, modulate(): return (normed * (1.0 + image_mod[1]) + image_mod[0]).astype(jnp.bfloat16)  6.3 us
  transfers between devices with their start and end apart: 5, of which 2 were waited for; matrix products, arithmetic and copies ran while one was open for 21% of the time, Pallas kernels for 0%

commit v1 on v0

--- a/solution.py
+++ b/solution.py
@@ -7,6 +7,12 @@
 GN_GROUPS = 32
 CHUNK = 512
 eps_norm = 1e-06
+
+
+def ends_guide(x_part):
+    for src_i in ("head", "seq"):
+        x_part = lax.psum(x_part, axis_name=src_i)
+    return x_part
 
 
 def group_gather(piece, group, dim):
@@ -31,7 +37,7 @@
         [jnp.sum(values, axis=(0, 1, 2)), jnp.sum(values * values, axis=(0, 1, 2))]
     )
     sums = jnp.sum(chan_sums.reshape(2, GN_GROUPS, per_group), axis=2)
-    sums = lax.psum(sums, ("seq", "head"))
+    sums = ends_guide(sums)
     cell_count = (
         frame_count
         * row_count

time: 297 us -> 285 us (0.960)
  blocking collectives: 169 us -> 158 us
    psum x1 -> x2, blocking collectives: 83.9 us -> 63.8 us  [ends_guide(): x_part = lax.psum(x_part, axis_name=src_i)]
    all_gather x1, blocking collectives: 68.1 us -> 76.6 us  [all_patches(): parts = lax.all_gather(flat, ('seq', 'head'), axis=0, tiled=False)]
  transfers between devices with their start and end apart: 5 -> 5, of which waited for: 2 -> 2; matrix products, arithmetic and copies ran while one was open for 21% -> 22% of each run, Pallas kernels for 0% -> 0%
where the time goes in v1:
time: 285 us
  blocking collectives  158 us (55%)
  matrix products  37.4 us (13%)
  local copies, waits for them, and re-layouts  29.8 us (10%)
  other arithmetic  21.1 us (7%)
  between operations  14.6 us (5%)
  waiting for transfers between devices  12.4 us (4%)
  starting transfers between devices  11.4 us (4%)
    all_gather x1, blocking collectives, all_patches(): parts = lax.all_gather(flat, ('seq', 'head'), axis=0, tiled=False)  76.6 us
    psum x2, blocking collectives, ends_guide(): x_part = lax.psum(x_part, axis_name=src_i)  63.8 us
    all_gather x1, blocking collectives, body(): mod = lax.all_gather(text_mod, 'seq', axis=1, tiled=True)  17.4 us
    dot_general x1, matrix products, body(): jnp.dot(text_table, chosen, preferred_element_type=jnp.float32)  9.17 us
    all_to_all x1, starting transfers between devices, body(): both = lax.all_to_all(both, 'seq', split_axis=0, concat_axis=0, tiled=True)  7.4 us
    reshape x2, local copies, waits for them, and re-layouts, body(): both = both.reshape(seq_n * depth, 5, cols)  6.86 us
    all_to_all x1, waiting for transfers between devices, body(): lax.all_to_all(attended, 'seq', split_axis=0, concat_axis=0, tiled=True)  6.85 us
    convert_element_type x1, other arithmetic, modulate(): return (normed * (1.0 + image_mod[1]) + image_mod[0]).astype(jnp.bfloat16)  6.31 us
  transfers between devices with their start and end apart: 5, of which 2 were waited for; matrix products, arithmetic and copies ran while one was open for 22% of the time, Pallas kernels for 0%

profile of v1, /device:TPU:0, one launch (start us, length us, event | category | flops | bytes accessed | tf_op | source)
XLA Modules:
  0.0 284.5 jit_solution(480143218326398796)
XLA Ops:
  6.5 2.5 copy.83
  9.0 1.6 copy.82
  10.7 0.4 pad_maximum_fusion
  11.1 0.2 copy.84
  11.3 2.6 copy.85
  14.0 7.4 %all-to-all-start = ((bf16[16,192,320]{2,1,0:T(8,128)(2,1)}), bf16[16,192,320]{2,1,0:T(8,128)(2,1)}, u32[]{:S(2)}, u32[]{:S(2)}) async-start(bf16[16,192,320]{2,1,0:T(8,128)(2,1)} %copy.85), calls=%async_computation | async-start | bytes 4718592 | tf_op jit(solution)/shard_map/all_to_all | solution.py:138
  21.4 0.0 all-gather.3.cloned.1.call-start
  21.5 9.2 %fusion.23 = bf16[192,512]{1,0:T(8,128)(2,1)} fusion(bf16[192,16384]{1,0:T(8,128)(2,1)} %param.27, s32[512]{0:T(512)S(1)} %copy-done.19), kind=kOutput, calls=%fused_computation.34 | convolution fusion | flops 3229712384 | bytes 6490112 | tf_op jit(solution)/shard_map/dot_general | solution.py:145
  30.7 0.1 convert_reduce_fusion.1
  30.8 0.1 stack.10
  30.9 0.1 stack.9
  30.9 0.1 maximum_reduce_fusion
  31.0 4.9 %psum.14 = f32[2,32]{1,0:T(2,128)S(1)} all-reduce(f32[2,32]{1,0:T(2,128)S(1)} %maximum_reduce_fusion), channel_id=1, replica_groups=mesh['seq'=16,'head'=2] {'head'}, use_global_device_ids=true, to_apply=%region_3.4 | all-reduce | flops 64 | bytes 512 | tf_op jit(solution)/shard_map/psum | solution.py:14
  36.0 58.8 %psum.15 = f32[2,32]{1,0:T(2,128)S(1)} all-reduce(f32[2,32]{1,0:T(2,128)S(1)} %psum.14), channel_id=1, replica_groups=mesh['seq'=16,'head'=2] {'seq'}, use_global_device_ids=true, to_apply=%region_4.5 | all-reduce | flops 64 | bytes 512 | tf_op jit(solution)/shard_map/psum | solution.py:14
  94.8 0.1 broadcast_in_dim.15
  94.9 0.1 mul.93
  95.0 0.1 broadcast_in_dim.14
  95.0 0.1 sub.50
  95.1 0.1 fusion.50
  95.3 0.1 maximum_bitcast_fusion.2
  95.3 4.2 %convolution_reduce_fusion = f32[8,4,6,16]{3,2,1,0:T(8,128)S(1)} fusion(bf16[3,3,3,16,512]{4,3,2,1,0:T(8,128)(2,1)S(1)} %copy-done, bf16[1,10,2,4,512]{4,3,2,1,0:T(4,128)(2,1)S(1)} %maximum_bitcast_fusion.2), kind=kOutput, calls=%fused_computation.36 | convolution fusion | flops 28311552 | bytes 536576 | tf_op jit(solution)/shard_map/conv_general_dilated | solution.py:79
  99.6 0.1 all_gather_reshape_squeeze.3
  99.7 76.6 %all_gather.9 = f32[32,24,128]{2,1,0:T(8,128)S(1)} all-gather(f32[1,24,128]{2,1,0:T(8,128)S(1)} %all_gather_reshape_squeeze.3), channel_id=1, replica_groups=mesh['seq'=16,'head'=2] {'seq','head'}, dimensions={0}, use_global_device_ids=true | all-gather | bytes 405504 | tf_op jit(solution)/shard_map/all_gather | solution.py:88
  176.3 0.3 reshape.98
  176.7 0.1 slice.94
  176.8 0.1 add.181
  176.9 0.2 fusion.65
  177.1 0.1 fusion.68
  177.2 0.2 fusion.34
  177.4 0.1 reshape.99
  177.6 0.3 copy.81
  177.8 0.1 reshape.100
  178.0 3.6 %add_reduce_fusion = (f32[512]{0:T(512)S(1)}, f32[512,3072]{1,0:T(8,128)}) fusion(f32[3072]{0:T(1024)S(1)} %copy-done.11, bf16[512,64]{1,0:T(8,128)(2,1)S(1)} %reshape.100, bf16[64,3072]{1,0:T(8,128)(2,1)S(1)} %copy-done.7), kind=kOutput, calls=%fused_computation.15 | convolution fusion | flops 204471808 | bytes 6764544 | tf_op jit(solution)/shard_map/dot_general | solution.py:101
  181.7 17.4 %all-gather = f32[16,192,2]{1,2,0:T(2,128)S(1)} all-gather(f32[1,192,2]{1,2,0:T(2,128)S(1)} %bitcast.101), channel_id=1, replica_groups=mesh['seq'=16,'head'=2] {'seq'}, dimensions={0}, use_global_device_ids=true | all-gather | bytes 26112 | tf_op jit(solution)/shard_map/all_gather | solution.py:149
  199.1 0.1 reshape.110
  199.2 3.9 %copy.86 = bf16[16,192,320]{1,0,2:T(8,128)(2,1)S(1)} copy(bf16[16,192,320]{2,1,0:T(8,128)(2,1)} %all-to-all-done) | data formatting | bytes 3932160 | tf_op jit(solution)/shard_map/all_to_all | solution.py:138
  203.1 3.8 %reshape.103 = bf16[3072,5,64]{0,2,1:T(8,128)(2,1)} reshape(bf16[16,192,320]{1,0,2:T(8,128)(2,1)S(1)} %copy.86) | data formatting | bytes 3932160 | tf_op jit(solution)/shard_map/reshape | solution.py:139
  206.9 0.3 collective-permute-start
  207.2 3.7 %multiply_reduce_fusion = f32[512]{0:T(512)S(1)} fusion(f32[512,3072]{1,0:T(8,128)} %get-tuple-element.29, f32[512]{0:T(512)S(1)} %broadcast_multiply_fusion.1, f32[3072]{0:T(1024)S(1)} %copy-done.11), kind=kLoop, calls=%fused_computation.14 | loop fusion | flops 6290944 | bytes 6307840 | tf_op jit(solution)/shard_map/reduce_sum | solution.py:104
  211.7 6.3 %add_convert_fusion = bf16[512,3072]{1,0:T(8,128)(2,1)} fusion(f32[512,3072]{1,0:T(8,128)} %get-tuple-element.29, f32[3072]{0:T(1024)S(1)} %bitcast.95, f32[3072]{0:T(1024)S(1)} %bitcast.96, f32[512]{0:T(512)S(1)} %add_rsqrt_fusion.1, f32[512]{0:T(512)S(1)} %broadcast_multiply_fusion.1, f32[3072]{0:T(1024)S(1)} %copy-done.11), kind=kLoop, calls=%fused_computation.13 | loop fusion | flops 9437184 | bytes 9478144 | tf_op jit(solution)/shard_map/convert_element_type | solution.py:106
  218.0 3.1 %copy.87 = bf16[3072,5,64]{2,0,1:T(8,128)(2,1)} copy(bf16[3072,5,64]{0,2,1:T(8,128)(2,1)S(1)} %copy-done.5) | data formatting | bytes 3932160 | tf_op jit(solution)/shard_map/reshape | solution.py:139
  221.1 4.7 %copy.88 = bf16[3072,5,64]{2,0,1:T(8,128)(2,1)} copy(bf16[3072,5,64]{0,2,1:T(8,128)(2,1)} %collective-permute-done) | data formatting | bytes 3932160 | tf_op jit(solution)/shard_map/ppermute | solution.py:23
  225.8 3.6 %broadcast_select_fusion.1 = (bf16[3072,5,64]{2,0,1:T(8,128)(2,1)S(1)}, bf16[3072,5,64]{2,0,1:T(8,128)(2,1)S(1)}) fusion(bf16[3072,5,64]{2,0,1:T(8,128)(2,1)} %copy.87, bf16[3072,5,64]{2,0,1:T(8,128)(2,1)} %copy.88, pred[]{:T(512)S(6)} %eq.14), kind=kLoop, calls=%fused_computation.17 | loop fusion | flops 1966080 | bytes 7864321 | tf_op jit(solution)/shard_map/jit(_where)/select_n | solution.py:26
  229.4 3.3 %pad_maximum_fusion.2 = (bf16[3072,2,128]{2,0,1:T(8,128)(2,1)S(1)}, bf16[3072,2,128]{2,0,1:T(8,128)(2,1)}) fusion(bf16[3072,5,64]{2,0,1:T(8,128)(2,1)S(1)} %get-tuple-element.12, bf16[3072,5,64]{2,0,1:T(8,128)(2,1)S(1)} %get-tuple-element.11), kind=kLoop, calls=%fused_computation.27 | loop fusion | flops 6291456 | bytes 7077888 | tf_op jit(solution)/shard_map/slice | solution.py:141
  232.8 0.2 copy-done.3
  232.9 2.6 copy.93
  235.5 1.6 copy.91
  237.1 3.5 %fusion.27 = bf16[16,2,16,128]{3,2,1,0:T(8,128)(2,1)S(1)} fusion(bf16[16,2,16,3072]{3,2,1,0:T(8,128)(2,1)} %bitcast.80, bf16[3072,5,64]{2,0,1:T(8,128)(2,1)} %copy-done.3, bf16[3072,5,64]{2,0,1:T(8,128)(2,1)} %copy-done.2), kind=kOutput, calls=%fused_computation.42 | convolution fusion | flops 404226048 | bytes 7208960 | tf_op jit(solution)/shard_map/dot_general | solution.py:177
  240.7 0.2 copy-done.9
  240.9 1.0 convolution_convert_fusion
  241.9 0.0 all-gather.3.cloned.1.call-done
  242.0 2.8 convert_reduce_fusion
  244.8 4.0 %fusion.43 = f32[512,256]{1,0:T(8,128)S(1)} fusion(bf16[3072,256]{0,1:T(8,128)(2,1)S(1)} %bitcast.83, bf16[3072,512]{1,0:T(8,128)(2,1)} %all-gather.3.cloned.1.call-done, f32[3072]{0:T(1024)S(1)} %bitcast.99, f32[3072]{0:T(1024)S(1)} %bitcast.97, f32[512]{0:T(512)S(1)} %get-tuple-element.27, f32[512]{0:T(512)S(1)} %get-tuple-element.26), kind=kOutput, calls=%fused_computation.58 | convolution fusion | flops 814743552 | bytes 5271552 | tf_op jit(solution)/shard_map/dot_general | solution.py:159
  248.8 2.1 fusion.19
  250.9 0.4 fusion.70
  251.3 0.3 fusion.25
  251.6 1.0 fusion.24
  252.6 3.6 %all-to-all-start.1 = ((bf16[16,16,128]{2,1,0:T(8,128)(2,1)}), bf16[16,16,128]{2,1,0:T(8,128)(2,1)S(1)}, u32[]{:S(2)}, u32[]{:S(2)}) async-start(bf16[16,16,128]{2,1,0:T(8,128)(2,1)} %bitcast.24), calls=%async_computation.1 | async-start | bytes 131072 | tf_op jit(solution)/shard_map/all_to_all | solution.py:203
  256.2 6.8 %all-to-all-done.1 = bf16[16,16,128]{2,1,0:T(8,128)(2,1)S(1)} async-done(((bf16[16,16,128]{2,1,0:T(8,128)(2,1)}), bf16[16,16,128]{2,1,0:T(8,128)(2,1)S(1)}, u32[]{:S(2)}, u32[]{:S(2)}) %all-to-all-start.1) | async-done | bytes 65568 | tf_op jit(solution)/shard_map/all_to_all | solution.py:203
  263.1 3.8 %fusion.51 = f32[16,3072]{1,0:T(8,128)S(1)} fusion(bf16[1024,3072]{1,0:T(8,128)(2,1)} %param.30, bf16[2,16,1024]{2,1,0:T(8,128)(2,1)S(1)} %bitcast.89, s32[]{:T(128)S(6)} %select_n.47), kind=kOutput, calls=%fused_computation.73 | convolution fusion | flops 100663296 | bytes 6520836 | tf_op jit(solution)/shard_map/dot_general | solution.py:208
  266.9 0.9 convolution_add_fusion
  267.7 5.5 %collective-permute-done.1 = f32[16,3072]{1,0:T(8,128)S(1)} collective-permute-done((f32[16,3072]{1,0:T(8,128)S(1)}, f32[16,3072]{1,0:T(8,128)S(1)}, u32[]{:S(2)}, u32[]{:S(2)}) %collective-permute-start.1) | collective-permute-done | bytes 196640 | tf_op jit(solution)/shard_map/ppermute | solution.py:218
  273.3 3.7 %fusion.12 = bf16[16,3072]{1,0:T(8,128)(2,1)S(1)} fusion(f32[16,3072]{1,0:T(8,128)S(1)} %convolution_add_fusion, f32[16,3072]{1,0:T(8,128)S(1)} %collective-permute-done.1, bf16[1024,3072]{1,0:T(8,128)(2,1)} %param.30, f32[3072]{0:T(1024)S(1)} %copy-done.14, f32[3072]{0:T(1024)S(1)} %bitcast.94, bf16[2,16,1024]{2,1,0:T(8,128)(2,1)S(1)} %bitcast.90, ...), kind=kOutput, calls=%fused_computation.23 | convolution fusion | flops 100909056 | bytes 6840324 | tf_op jit(solution)/shard_map/dot_general | solution.py:213
  277.0 0.7 reshape.108
  (58 shorter events, 0.3 us)
Async XLA Ops:
  6.5 88.8 %copy-start = (bf16[3,3,3,16,512]{4,3,2,1,0:T(8,128)(2,1)S(1)}, bf16[3,3,3,16,512]{4,3,2,1,0:T(8,128)(2,1)}, u32[]{:S(2)}) copy-start(bf16[3,3,3,16,512]{4,3,2,1,0:T(8,128)(2,1)} %param.19) | copy-start | bytes 1327108
  11.3 10.2 %copy-start.19 = (s32[512]{0:T(512)S(1)}, s32[512]{0:T(512)}, u32[]{:S(2)}) copy-start(s32[512]{0:T(512)} %param.25) | copy-start | bytes 6148
  14.0 185.2 %all-to-all-start = ((bf16[16,192,320]{2,1,0:T(8,128)(2,1)}), bf16[16,192,320]{2,1,0:T(8,128)(2,1)}, u32[]{:S(2)}, u32[]{:S(2)}) async-start(bf16[16,192,320]{2,1,0:T(8,128)(2,1)} %copy.85), calls=%async_computation | async-start | bytes 4718592 | tf_op jit(solution)/shard_map/all_to_all | solution.py:138
  21.4 9.3 %copy-start.12 = (bf16[8,2,4,512]{3,2,1,0:T(4,128)(2,1)S(1)}, bf16[8,2,4,512]{3,2,1,0:T(4,128)(2,1)}, u32[]{:S(2)}) copy-start(bf16[8,2,4,512]{3,2,1,0:T(4,128)(2,1)} %param.16) | copy-start | bytes 196612
  21.4 73.7 %copy-start.15 = (f32[512]{0:T(512)S(1)}, f32[512]{0:T(512)}, u32[]{:S(2)}) copy-start(f32[512]{0:T(512)} %param.18) | copy-start | bytes 6148
  21.4 73.7 %copy-start.16 = (f32[512]{0:T(512)S(1)}, f32[512]{0:T(512)}, u32[]{:S(2)}) copy-start(f32[512]{0:T(512)} %param.17) | copy-start | bytes 6148
  21.4 155.4 %copy-start.18 = (f32[16]{0:T(128)S(1)}, f32[16]{0:T(128)}, u32[]{:S(2)}) copy-start(f32[16]{0:T(128)} %param.20) | copy-start | bytes 196
  21.4 220.5 %all-gather.3.cloned.1.call-start = ((), (), s32[]{:S(2)}) async-start(), calls=%async_computation.2 | async-start | bytes 3342336 | tf_op jit(solution)/shard_map/all_gather | solution.py:148
  30.7 147.3 %copy-start.7 = (bf16[64,3072]{1,0:T(8,128)(2,1)S(1)}, bf16[64,3072]{1,0:T(8,128)(2,1)}, u32[]{:S(2)}) copy-start(bf16[64,3072]{1,0:T(8,128)(2,1)} %param.21) | copy-start | bytes 1179652
  30.7 147.3 %copy-start.11 = (f32[3072]{0:T(1024)S(1)}, f32[3072]{0:T(1024)}, u32[]{:S(2)}) copy-start(f32[3072]{0:T(1024)} %param.22) | copy-start | bytes 36868
  178.0 3.6 %copy-start.10 = (bf16[512,64]{1,0:T(8,128)(2,1)}, bf16[512,64]{1,0:T(8,128)(2,1)S(1)}, u32[]{:S(2)}) copy-start(bf16[512,64]{1,0:T(8,128)(2,1)S(1)} %reshape.100) | copy-start | bytes 196612
  178.0 3.6 %copy-start.17 = (f32[2,192]{1,0:T(2,128)S(1)}, f32[2,192]{1,0:T(2,128)}, u32[]{:S(2)}) copy-start(f32[2,192]{1,0:T(2,128)} %param.28) | copy-start | bytes 4612
  206.9 4.7 %copy-start.13 = (f32[3,3072]{1,0:T(4,128)S(1)}, f32[3,3072]{1,0:T(4,128)}, u32[]{:S(2)}) copy-start(f32[3,3072]{1,0:T(4,128)} %param.23) | copy-start | bytes 110596
  206.9 14.2 %collective-permute-start = (bf16[3072,5,64]{0,2,1:T(8,128)(2,1)}, bf16[3072,5,64]{0,2,1:T(8,128)(2,1)}, u32[]{:S(2)}, u32[]{:S(2)}) collective-permute-start(bf16[3072,5,64]{0,2,1:T(8,128)(2,1)} %reshape.103), channel_id=1, source_target_pairs={{0,2},{2,0},{4,6},{6,4},{8,10},{10,8},{12,14},{14,12},{16,18},{18,... | collective-permute-start | bytes 5898248 | tf_op jit(solution)/shard_map/ppermute | solution.py:23
  211.7 6.3 %copy-start.5 = (bf16[3072,5,64]{0,2,1:T(8,128)(2,1)S(1)}, bf16[3072,5,64]{0,2,1:T(8,128)(2,1)}, u32[]{:S(2)}) copy-start(bf16[3072,5,64]{0,2,1:T(8,128)(2,1)} %reshape.103) | copy-start | bytes 5898244
  229.4 3.4 %copy-start.2 = (bf16[3072,5,64]{2,0,1:T(8,128)(2,1)}, bf16[3072,5,64]{2,0,1:T(8,128)(2,1)S(1)}, u32[]{:S(2)}) copy-start(bf16[3072,5,64]{2,0,1:T(8,128)(2,1)S(1)} %get-tuple-element.11) | copy-start | bytes 5898244
  229.4 3.5 %copy-start.3 = (bf16[3072,5,64]{2,0,1:T(8,128)(2,1)}, bf16[3072,5,64]{2,0,1:T(8,128)(2,1)S(1)}, u32[]{:S(2)}) copy-start(bf16[3072,5,64]{2,0,1:T(8,128)(2,1)S(1)} %get-tuple-element.12) | copy-start | bytes 5898244
  237.1 3.6 %copy-start.4 = (bf16[512,3072]{1,0:T(8,128)(2,1)S(1)}, bf16[512,3072]{1,0:T(8,128)(2,1)}, u32[]{:S(2)}) copy-start(bf16[512,3072]{1,0:T(8,128)(2,1)} %add_convert_fusion) | copy-start | bytes 9437188
  237.1 3.8 %copy-start.9 = (bf16[3072,2,128]{0,2,1:T(8,128)(2,1)S(1)}, bf16[3072,2,128]{0,2,1:T(8,128)(2,1)}, u32[]{:S(2)}) copy-start(bf16[3072,2,128]{0,2,1:T(8,128)(2,1)} %copy.91) | copy-start | bytes 4718596
  240.9 3.9 %copy-start.8 = (bf16[3072,2,128]{0,2,1:T(8,128)(2,1)S(1)}, bf16[3072,2,128]{0,2,1:T(8,128)(2,1)}, u32[]{:S(2)}) copy-start(bf16[3072,2,128]{0,2,1:T(8,128)(2,1)} %copy.93) | copy-start | bytes 4718596
  244.7 4.0 %copy-start.6 = (bf16[3072,512]{1,0:T(8,128)(2,1)S(1)}, bf16[3072,512]{1,0:T(8,128)(2,1)}, u32[]{:S(2)}) copy-start(bf16[3072,512]{1,0:T(8,128)(2,1)} %all-gather.3.cloned.1.call-done) | copy-start | bytes 9437188
  252.6 20.7 %copy-start.14 = (f32[3072]{0:T(1024)S(1)}, f32[3072]{0:T(1024)}, u32[]{:S(2)}) copy-start(f32[3072]{0:T(1024)} %param.31) | copy-start | bytes 36868
  252.6 10.5 %all-to-all-start.1 = ((bf16[16,16,128]{2,1,0:T(8,128)(2,1)}), bf16[16,16,128]{2,1,0:T(8,128)(2,1)S(1)}, u32[]{:S(2)}, u32[]{:S(2)}) async-start(bf16[16,16,128]{2,1,0:T(8,128)(2,1)} %bitcast.24), calls=%async_computation.1 | async-start | bytes 131072 | tf_op jit(solution)/shard_map/all_to_all | solution.py:203
  263.1 14.6 %copy-start.1 = (bf16[3,3,3,16,512]{4,3,2,1,0:T(8,128)(2,1)S(1)}, bf16[3,3,3,16,512]{4,3,2,1,0:T(8,128)(2,1)}, u32[]{:S(2)}) copy-start(bf16[3,3,3,16,512]{4,3,2,1,0:T(8,128)(2,1)} %param.19) | copy-start | bytes 1327108
  266.9 6.4 %collective-permute-start.1 = (f32[16,3072]{1,0:T(8,128)S(1)}, f32[16,3072]{1,0:T(8,128)S(1)}, u32[]{:S(2)}, u32[]{:S(2)}) collective-permute-start(f32[16,3072]{1,0:T(8,128)S(1)} %fusion.51), channel_id=1, source_target_pairs={{0,1},{1,0},{2,3},{3,2},{4,5},{5,4},{6,7},{7,6},{8,9},{9,8},{10,11... | collective-permute-start | bytes 589832 | tf_op jit(solution)/shard_map/ppermute | solution.py:218
Sparse Core Ops, SparseCore 0:
  30.8 65.9 all-gather.2
